TPU v7x, 32 devices: a whole 2x2x4 slice. The times are simulated.
32 devices in a mesh: row: 4 (over y, x), col: 8 (over z, core).
Axes of the slice: x: 2, y: 2, z: 4, core: 2. Of those that a mesh axis runs over, the one named last changes fastest.
Arguments:
- hist_corr: float32 [16384, 16384], P('row', 'col'), may hold values from -1 to 1
- hist_resp: float32 [16384, 16384], P('row', 'col'), may hold values from -1 to 1, as said below
- row_corr: float32 [128, 16384], P(None, 'col'), may hold values from -1 to 1
- row_resp: float32 [128, 16384], P(None, 'col'), may hold values from -1 to 1
Outputs:
- final_corr: float32 [128, 16384], P(None, 'col')
- final_resp: float32 [128, 16384], P(None, 'col')
Inputs may be any that keep to these rules, and one draw needn't show every extreme that they name: hist_resp[s, u] is 0 where u > s and 1 where u == s.
All inputs are finite; a program needn't handle non-finite values.
Results may differ from a plain program's by a relative error of at most 0.00015.
Values sent between devices are 32-bit elements; how exact they have to be, the bound alone decides.
A program may use at most 128 MiB of HBM per device.

v0:
```python
import math
import jax
import jax.numpy as jnp
from jax import lax
from jax.sharding import PartitionSpec as P

HIST = 16384
BLOCKS = 4
step_size = 0.2
heat_reservoir_warmth = 0.6


def turn_rows(values):
    row_count = lax.axis_size("row")
    col_count = lax.axis_size("col")
    my_row = lax.axis_index("row")
    piece_span = values.shape[1] // row_count
    piece = lax.dynamic_slice_in_dim(values, my_row * piece_span, piece_span, 1)
    spread = jnp.broadcast_to(piece[None, None], (col_count, 1) + piece.shape)
    moved = lax.all_to_all(
        lax.all_to_all(spread, "col", split_axis=0, concat_axis=1, tiled=True),
        "row",
        split_axis=1,
        concat_axis=0,
        tiled=True,
    )
    return jnp.transpose(moved, (2, 1, 0, 3)).reshape(piece.shape[0], -1)


def turn_cols(values):
    row_count = lax.axis_size("row")
    col_count = lax.axis_size("col")
    my_col = lax.axis_index("col")
    factor = col_count // row_count
    block_span = values.shape[1] // factor
    piece_span = block_span // col_count
    blocks = values.reshape(values.shape[0], factor, block_span)
    piece = lax.dynamic_slice_in_dim(blocks, my_col * piece_span, piece_span, 2)
    ordered = jnp.transpose(piece, (1, 0, 2))
    spread = jnp.broadcast_to(ordered[None], (row_count,) + ordered.shape)
    moved = lax.all_to_all(
        lax.all_to_all(spread, "row", split_axis=0, concat_axis=1, tiled=True),
        "col",
        split_axis=1,
        concat_axis=0,
        tiled=True,
    )
    return jnp.transpose(moved[:, 0], (1, 0, 2)).reshape(values.shape[0], -1)


def energy_layout(values):
    return turn_rows(values)


def cross_layout(values):
    return turn_cols(values)


def advance(
    autocovariance_curve,
    perturbation_reaction,
    memory_corr,
    memory_resp,
    cross_term,
    norm_enforcing_scalar,
    integration_coefficient,
):
    next_corr = autocovariance_curve + step_size * (
        integration_coefficient * (memory_corr + cross_term)
        - norm_enforcing_scalar * autocovariance_curve
    )
    next_resp = perturbation_reaction + step_size * (
        integration_coefficient * memory_resp - norm_enforcing_scalar * perturbation_reaction
    )
    return (next_corr, next_resp)


def body(hist_corr, hist_resp, row_corr, row_resp):
    highest = lax.Precision.HIGHEST
    integration_coefficient = 1.0 / math.sqrt(HIST)
    autocovariance_curve = row_corr
    perturbation_reaction = row_resp
    for block_index in range(BLOCKS):
        history_integrand = 3.0 * autocovariance_curve * perturbation_reaction
        slope_contribution = 1.5 * autocovariance_curve * autocovariance_curve
        multiplier_terms = jnp.sum(
            history_integrand * autocovariance_curve + slope_contribution * perturbation_reaction,
            axis=1,
        )
        part_cross = lax.dot_general(
            slope_contribution,
            hist_resp,
            (((1,), (1,)), ((), ())),
            precision=highest,
            preferred_element_type=jnp.float32,
        )
        enforcing_scalar_sum = lax.psum(multiplier_terms, "col")
        energy_rows = energy_layout(history_integrand)
        cross_total = lax.psum(part_cross, "col")
        cross_term = cross_layout(cross_total)
        norm_enforcing_scalar = (
            heat_reservoir_warmth + integration_coefficient * enforcing_scalar_sum[:, None]
        )
        part_corr = jnp.dot(
            energy_rows, hist_corr, precision=highest, preferred_element_type=jnp.float32
        )
        part_resp = jnp.dot(
            energy_rows, hist_resp, precision=highest, preferred_element_type=jnp.float32
        )
        memory_corr, memory_resp = lax.psum((part_corr, part_resp), "row")
        autocovariance_curve, perturbation_reaction = advance(
            autocovariance_curve,
            perturbation_reaction,
            memory_corr,
            memory_resp,
            cross_term,
            norm_enforcing_scalar,
            integration_coefficient,
        )
    return (autocovariance_curve, perturbation_reaction)


def solution(mesh):
    in_specs = (P("row", "col"), P("row", "col"), P(None, "col"), P(None, "col"))
    out_specs = (P(None, "col"), P(None, "col"))
    return jax.shard_map(body, mesh=mesh, in_specs=in_specs, out_specs=out_specs, check_vma=False)
```

profile of v0, /device:TPU:0, one launch (start us, length us, event | category | flops | bytes accessed | tf_op | source)
XLA Modules:
  0.0 1180.2 jit_solution(5139241333706496647)
XLA Ops:
  10.2 55.3 %all_to_all.180 = f32[8,1,128,512]{3,2,1,0:T(8,128)} all-to-all(f32[8,1,128,512]{3,2,1,0:T(8,128)S(1)} %broadcast_in_dim.16), channel_id=1, replica_groups=mesh['row'=4,'col'=8] {'col'}, dimensions={0} | all-to-all | bytes 4194304 | tf_op jit(solution)/shard_map/all_to_all | solution.py:21
  65.5 4.6 all-to-all-start.1
  70.1 37.2 %fusion = f32[128,4096]{1,0:T(8,128)S(1)} fusion(f32[4096,2048]{1,0:T(8,128)} %param.5, f32[128,2048]{1,0:T(8,128)S(1)} %copy-done.4), kind=kOutput, calls=%fused_computation.20 | convolution fusion | flops 12885426176 | bytes 36700160 | tf_op jit(solution)/shard_map/dot_general | solution.py:90
  110.3 64.6 %all-reduce.13.cloned.1.call-done = f32[128,2,2048]{2,1,0:T(2,128)} async-done(((f32[128,2,2048]{2,1,0:T(2,128)}), f32[128,2,2048]{2,1,0:T(2,128)}) %all-reduce.13.cloned.1.call-update) | async-done | bytes 2097168 | tf_op jit(solution)/shard_map/psum | solution.py:99
  183.6 22.4 %fusion.13 = f32[128,2048]{1,0:T(8,128)} fusion(f32[128,4096]{0,1:T(8,128)S(1)} %bitcast.88, f32[4096,2048]{1,0:T(8,128)} %param.5), kind=kOutput, calls=%fused_computation.45 | convolution fusion | flops 12884901888 | bytes 36700160 | tf_op jit(solution)/shard_map/dot_general | solution.py:107
  206.0 22.4 %fusion.12 = f32[128,2048]{1,0:T(8,128)} fusion(f32[128,4096]{0,1:T(8,128)S(1)} %bitcast.89, f32[4096,2048]{1,0:T(8,128)} %param.4), kind=kOutput, calls=%fused_computation.44 | convolution fusion | flops 12884901888 | bytes 36700160 | tf_op jit(solution)/shard_map/dot_general | solution.py:104
  234.3 29.3 %psum.114 = f32[128]{0:T(128)S(1)} all-reduce(f32[128]{0:T(128)S(1)} %get-tuple-element.20), channel_id=1, replica_groups=mesh['row'=4,'col'=8] {'col'}, use_global_device_ids=true, to_apply=%region_3.0 | all-reduce | flops 128 | bytes 1024 | tf_op jit(solution)/shard_map/psum | solution.py:97
  264.8 33.0 %all-reduce.27.cloned.1.call-done = (f32[128,2048]{1,0:T(8,128)}, f32[128,2048]{1,0:T(8,128)}) async-done(((f32[128,2048]{1,0:T(8,128)}, f32[128,2048]{1,0:T(8,128)}), (f32[128,2048]{1,0:T(8,128)}, f32[128,2048]{1,0:T(8,128)})) %all-reduce.27.cloned.1.call-update) | async-done | bytes 2097168 | tf_op jit(solution)/shard_map/psum | solution.py:110
  301.2 53.5 %all_to_all.181 = f32[8,1,128,512]{3,2,1,0:T(8,128)} all-to-all(f32[8,1,128,512]{3,2,1,0:T(8,128)S(1)} %broadcast_in_dim.18), channel_id=1, replica_groups=mesh['row'=4,'col'=8] {'col'}, dimensions={0} | all-to-all | bytes 4194304 | tf_op jit(solution)/shard_map/all_to_all | solution.py:21
  354.8 4.5 all-to-all-start.5
  359.5 39.0 %fusion.1 = f32[128,4096]{1,0:T(8,128)} fusion(f32[4096,2048]{1,0:T(8,128)} %param.5, f32[128,2048]{1,0:T(8,128)S(1)} %get-tuple-element.18), kind=kOutput, calls=%fused_computation.21 | convolution fusion | flops 12885426176 | bytes 36700160 | tf_op jit(solution)/shard_map/dot_general | solution.py:90
  402.5 64.6 %all-reduce.15.cloned.1.call-done = f32[128,2,2048]{2,1,0:T(2,128)} async-done(((f32[128,2,2048]{2,1,0:T(2,128)}), f32[128,2,2048]{2,1,0:T(2,128)}) %all-reduce.15.cloned.1.call-update) | async-done | bytes 2097168 | tf_op jit(solution)/shard_map/psum | solution.py:99
  476.0 22.4 %fusion.15 = f32[128,2048]{1,0:T(8,128)} fusion(f32[128,4096]{0,1:T(8,128)S(1)} %bitcast.90, f32[4096,2048]{1,0:T(8,128)} %param.5), kind=kOutput, calls=%fused_computation.47 | convolution fusion | flops 12884901888 | bytes 36700160 | tf_op jit(solution)/shard_map/dot_general | solution.py:107
  498.4 22.4 %fusion.14 = f32[128,2048]{1,0:T(8,128)} fusion(f32[128,4096]{0,1:T(8,128)S(1)} %bitcast.91, f32[4096,2048]{1,0:T(8,128)} %param.4), kind=kOutput, calls=%fused_computation.46 | convolution fusion | flops 12884901888 | bytes 36700160 | tf_op jit(solution)/shard_map/dot_general | solution.py:104
  526.9 29.3 %psum.118 = f32[128]{0:T(128)S(1)} all-reduce(f32[128]{0:T(128)S(1)} %get-tuple-element.16), channel_id=1, replica_groups=mesh['row'=4,'col'=8] {'col'}, use_global_device_ids=true, to_apply=%region_8.0 | all-reduce | flops 128 | bytes 1024 | tf_op jit(solution)/shard_map/psum | solution.py:97
  557.3 32.9 %all-reduce.25.cloned.1.call-done = (f32[128,2048]{1,0:T(8,128)}, f32[128,2048]{1,0:T(8,128)}) async-done(((f32[128,2048]{1,0:T(8,128)}, f32[128,2048]{1,0:T(8,128)}), (f32[128,2048]{1,0:T(8,128)}, f32[128,2048]{1,0:T(8,128)})) %all-reduce.25.cloned.1.call-update) | async-done | bytes 2097168 | tf_op jit(solution)/shard_map/psum | solution.py:110
  593.9 53.5 %all_to_all.182 = f32[8,1,128,512]{3,2,1,0:T(8,128)} all-to-all(f32[8,1,128,512]{3,2,1,0:T(8,128)S(1)} %broadcast_in_dim.20), channel_id=1, replica_groups=mesh['row'=4,'col'=8] {'col'}, dimensions={0} | all-to-all | bytes 4194304 | tf_op jit(solution)/shard_map/all_to_all | solution.py:21
  647.4 4.5 all-to-all-start.9
  652.1 37.2 %fusion.2 = f32[128,4096]{1,0:T(8,128)S(1)} fusion(f32[4096,2048]{1,0:T(8,128)} %param.5, f32[128,2048]{1,0:T(8,128)S(1)} %get-tuple-element.15), kind=kOutput, calls=%fused_computation.22 | convolution fusion | flops 12885426176 | bytes 36700160 | tf_op jit(solution)/shard_map/dot_general | solution.py:90
  692.2 64.6 %all-reduce.17.cloned.1.call-done = f32[128,2,2048]{2,1,0:T(2,128)} async-done(((f32[128,2,2048]{2,1,0:T(2,128)}), f32[128,2,2048]{2,1,0:T(2,128)}) %all-reduce.17.cloned.1.call-update) | async-done | bytes 2097168 | tf_op jit(solution)/shard_map/psum | solution.py:99
  765.5 22.4 %fusion.17 = f32[128,2048]{1,0:T(8,128)} fusion(f32[128,4096]{0,1:T(8,128)S(1)} %bitcast.92, f32[4096,2048]{1,0:T(8,128)} %param.5), kind=kOutput, calls=%fused_computation.49 | convolution fusion | flops 12884901888 | bytes 36700160 | tf_op jit(solution)/shard_map/dot_general | solution.py:107
  788.0 22.4 %fusion.16 = f32[128,2048]{1,0:T(8,128)} fusion(f32[128,4096]{0,1:T(8,128)S(1)} %bitcast.93, f32[4096,2048]{1,0:T(8,128)} %param.4), kind=kOutput, calls=%fused_computation.48 | convolution fusion | flops 12884901888 | bytes 36700160 | tf_op jit(solution)/shard_map/dot_general | solution.py:104
  816.4 29.3 %psum.122 = f32[128]{0:T(128)S(1)} all-reduce(f32[128]{0:T(128)S(1)} %get-tuple-element.13), channel_id=1, replica_groups=mesh['row'=4,'col'=8] {'col'}, use_global_device_ids=true, to_apply=%region_13.0 | all-reduce | flops 128 | bytes 1024 | tf_op jit(solution)/shard_map/psum | solution.py:97
  846.9 32.9 %all-reduce.23.cloned.1.call-done = (f32[128,2048]{1,0:T(8,128)}, f32[128,2048]{1,0:T(8,128)}) async-done(((f32[128,2048]{1,0:T(8,128)}, f32[128,2048]{1,0:T(8,128)}), (f32[128,2048]{1,0:T(8,128)}, f32[128,2048]{1,0:T(8,128)})) %all-reduce.23.cloned.1.call-update) | async-done | bytes 2097168 | tf_op jit(solution)/shard_map/psum | solution.py:110
  883.4 53.5 %all_to_all.183 = f32[8,1,128,512]{3,2,1,0:T(8,128)} all-to-all(f32[8,1,128,512]{3,2,1,0:T(8,128)S(1)} %broadcast_in_dim.22), channel_id=1, replica_groups=mesh['row'=4,'col'=8] {'col'}, dimensions={0} | all-to-all | bytes 4194304 | tf_op jit(solution)/shard_map/all_to_all | solution.py:21
  936.9 4.5 all-to-all-start.13
  941.9 37.3 %fusion.3 = f32[128,4096]{1,0:T(8,128)S(1)} fusion(f32[4096,2048]{1,0:T(8,128)} %param.5, f32[128,2048]{1,0:T(8,128)S(1)} %get-tuple-element.12), kind=kOutput, calls=%fused_computation.23 | convolution fusion | flops 12885426176 | bytes 36700160 | tf_op jit(solution)/shard_map/dot_general | solution.py:90
  982.0 64.6 %all-reduce.19.cloned.1.call-done = f32[128,2,2048]{2,1,0:T(2,128)} async-done(((f32[128,2,2048]{2,1,0:T(2,128)}), f32[128,2,2048]{2,1,0:T(2,128)}) %all-reduce.19.cloned.1.call-update) | async-done | bytes 2097168 | tf_op jit(solution)/shard_map/psum | solution.py:99
  1054.6 22.4 %fusion.19 = f32[128,2048]{1,0:T(8,128)} fusion(f32[128,4096]{0,1:T(8,128)S(1)} %bitcast.94, f32[4096,2048]{1,0:T(8,128)} %param.5), kind=kOutput, calls=%fused_computation.51 | convolution fusion | flops 12884901888 | bytes 36700160 | tf_op jit(solution)/shard_map/dot_general | solution.py:107
  1077.0 22.4 %fusion.18 = f32[128,2048]{1,0:T(8,128)} fusion(f32[128,4096]{0,1:T(8,128)S(1)} %bitcast.95, f32[4096,2048]{1,0:T(8,128)} %param.4), kind=kOutput, calls=%fused_computation.50 | convolution fusion | flops 12884901888 | bytes 36700160 | tf_op jit(solution)/shard_map/dot_general | solution.py:104
  1104.3 29.3 %psum.126 = f32[128]{0:T(128)S(1)} all-reduce(f32[128]{0:T(128)S(1)} %get-tuple-element.10), channel_id=1, replica_groups=mesh['row'=4,'col'=8] {'col'}, use_global_device_ids=true, to_apply=%region_18.0 | all-reduce | flops 128 | bytes 1024 | tf_op jit(solution)/shard_map/psum | solution.py:97
  1134.7 34.2 %all-reduce.21.cloned.1.call-done = (f32[128,2048]{1,0:T(8,128)}, f32[128,2048]{1,0:T(8,128)}) async-done(((f32[128,2048]{1,0:T(8,128)}, f32[128,2048]{1,0:T(8,128)}), (f32[128,2048]{1,0:T(8,128)}, f32[128,2048]{1,0:T(8,128)})) %all-reduce.21.cloned.1.call-update) | async-done | bytes 2097168 | tf_op jit(solution)/shard_map/psum | solution.py:110
  (98 shorter events, 91.2 us)
Async XLA Ops:
  65.5 4.7 copy-start.4
  65.5 110.4 %all-to-all-start.1 = ((f32[1,8,128,512]{3,2,0,1:T(8,128)}), f32[1,8,128,512]{3,2,0,1:T(8,128)}, u32[]{:S(2)}, u32[]{:S(2)}) async-start(f32[1,8,128,512]{3,2,0,1:T(8,128)} %bitcast.1), calls=%async_computation.1 | async-start | bytes 4194304 | tf_op jit(solution)/shard_map/all_to_all | solution.py:20
  70.1 104.8 %all-reduce.13.cloned.1.call-start = ((), (), s32[]{:S(2)}) async-start(), calls=%async_computation.16 | async-start | bytes 4194304 | tf_op jit(solution)/shard_map/psum | solution.py:99
  177.2 51.3 %all-to-all-start.2 = ((f32[4,2,128,256]{3,1,2,0:T(2,128)}), f32[4,2,128,256]{3,1,2,0:T(2,128)}, u32[]{:S(2)}, u32[]{:S(2)}) async-start(f32[4,2,128,256]{3,1,2,0:T(2,128)} %broadcast_in_dim.17), calls=%async_computation.2 | async-start | bytes 2097152 | tf_op jit(solution)/shard_map/all_to_all | solution.py:42
  181.4 116.4 %all-reduce.27.cloned.1.call-start = ((), (), s32[]{:S(2)}) async-start(), calls=%async_computation.23 | async-start | bytes 4194304 | tf_op jit(solution)/shard_map/psum | solution.py:110
  230.8 32.9 %all-to-all-start.3 = ((f32[1,8,128,256]{3,2,0,1:T(8,128)}), f32[1,8,128,256]{3,2,0,1:T(8,128)S(1)}, u32[]{:S(2)}, u32[]{:S(2)}) async-start(f32[1,8,128,256]{3,2,0,1:T(8,128)} %bitcast.7), calls=%async_computation.3 | async-start | bytes 2097152 | tf_op jit(solution)/shard_map/all_to_all | solution.py:41
  300.8 58.7 %copy-start = (f32[128,2048]{1,0:T(8,128)}, f32[128,2048]{1,0:T(8,128)S(1)}, u32[]{:S(2)}) copy-start(f32[128,2048]{1,0:T(8,128)S(1)} %get-tuple-element.18) | copy-start | bytes 3145732
  354.8 113.3 %all-to-all-start.5 = ((f32[1,8,128,512]{3,2,0,1:T(8,128)}), f32[1,8,128,512]{3,2,0,1:T(8,128)}, u32[]{:S(2)}, u32[]{:S(2)}) async-start(f32[1,8,128,512]{3,2,0,1:T(8,128)} %bitcast.96), calls=%async_computation.5 | async-start | bytes 4194304 | tf_op jit(solution)/shard_map/all_to_all | solution.py:20
  359.2 107.9 %all-reduce.15.cloned.1.call-start = ((), (), s32[]{:S(2)}) async-start(), calls=%async_computation.17 | async-start | bytes 4194304 | tf_op jit(solution)/shard_map/psum | solution.py:99
  469.3 51.5 %all-to-all-start.6 = ((f32[4,2,128,256]{3,1,2,0:T(2,128)}), f32[4,2,128,256]{3,1,2,0:T(2,128)}, u32[]{:S(2)}, u32[]{:S(2)}) async-start(f32[4,2,128,256]{3,1,2,0:T(2,128)} %broadcast_in_dim.19), calls=%async_computation.6 | async-start | bytes 2097152 | tf_op jit(solution)/shard_map/all_to_all | solution.py:42
  473.6 116.6 %all-reduce.25.cloned.1.call-start = ((), (), s32[]{:S(2)}) async-start(), calls=%async_computation.22 | async-start | bytes 4194304 | tf_op jit(solution)/shard_map/psum | solution.py:110
  523.2 67.0 %copy-start.1 = (f32[128,2048]{1,0:T(8,128)S(1)}, f32[128,2048]{1,0:T(8,128)}, u32[]{:S(2)}) copy-start(f32[128,2048]{1,0:T(8,128)} %copy-done) | copy-start | bytes 3145732
  523.2 33.0 %all-to-all-start.7 = ((f32[1,8,128,256]{3,2,0,1:T(8,128)}), f32[1,8,128,256]{3,2,0,1:T(8,128)S(1)}, u32[]{:S(2)}, u32[]{:S(2)}) async-start(f32[1,8,128,256]{3,2,0,1:T(8,128)} %bitcast.101), calls=%async_computation.7 | async-start | bytes 2097152 | tf_op jit(solution)/shard_map/all_to_all | solution.py:41
  592.9 1.0 copy-start.5
  647.4 110.4 %all-to-all-start.9 = ((f32[1,8,128,512]{3,2,0,1:T(8,128)}), f32[1,8,128,512]{3,2,0,1:T(8,128)}, u32[]{:S(2)}, u32[]{:S(2)}) async-start(f32[1,8,128,512]{3,2,0,1:T(8,128)} %bitcast.21), calls=%async_computation.9 | async-start | bytes 4194304 | tf_op jit(solution)/shard_map/all_to_all | solution.py:20
  651.8 105.0 %all-reduce.17.cloned.1.call-start = ((), (), s32[]{:S(2)}) async-start(), calls=%async_computation.18 | async-start | bytes 4194304 | tf_op jit(solution)/shard_map/psum | solution.py:99
  759.1 51.3 %all-to-all-start.10 = ((f32[4,2,128,256]{3,1,2,0:T(2,128)}), f32[4,2,128,256]{3,1,2,0:T(2,128)}, u32[]{:S(2)}, u32[]{:S(2)}) async-start(f32[4,2,128,256]{3,1,2,0:T(2,128)} %broadcast_in_dim.21), calls=%async_computation.10 | async-start | bytes 2097152 | tf_op jit(solution)/shard_map/all_to_all | solution.py:42
  763.3 116.5 %all-reduce.23.cloned.1.call-start = ((), (), s32[]{:S(2)}) async-start(), calls=%async_computation.21 | async-start | bytes 4194304 | tf_op jit(solution)/shard_map/psum | solution.py:110
  812.7 67.0 %copy-start.6 = (f32[128,2048]{1,0:T(8,128)S(1)}, f32[128,2048]{1,0:T(8,128)}, u32[]{:S(2)}) copy-start(f32[128,2048]{1,0:T(8,128)} %copy-done.5) | copy-start | bytes 3145732
  812.7 33.0 %all-to-all-start.11 = ((f32[1,8,128,256]{3,2,0,1:T(8,128)}), f32[1,8,128,256]{3,2,0,1:T(8,128)S(1)}, u32[]{:S(2)}, u32[]{:S(2)}) async-start(f32[1,8,128,256]{3,2,0,1:T(8,128)} %bitcast.102), calls=%async_computation.11 | async-start | bytes 2097152 | tf_op jit(solution)/shard_map/all_to_all | solution.py:41
  882.4 1.0 copy-start.7
  882.4 59.4 %copy-start.2 = (f32[128,2048]{1,0:T(8,128)}, f32[128,2048]{1,0:T(8,128)S(1)}, u32[]{:S(2)}) copy-start(f32[128,2048]{1,0:T(8,128)S(1)} %get-tuple-element.12) | copy-start | bytes 3145732
  936.9 110.6 %all-to-all-start.13 = ((f32[1,8,128,512]{3,2,0,1:T(8,128)}), f32[1,8,128,512]{3,2,0,1:T(8,128)}, u32[]{:S(2)}, u32[]{:S(2)}) async-start(f32[1,8,128,512]{3,2,0,1:T(8,128)} %bitcast.31), calls=%async_computation.13 | async-start | bytes 4194304 | tf_op jit(solution)/shard_map/all_to_all | solution.py:20
  941.4 105.2 %all-reduce.19.cloned.1.call-start = ((), (), s32[]{:S(2)}) async-start(), calls=%async_computation.19 | async-start | bytes 4194304 | tf_op jit(solution)/shard_map/psum | solution.py:99
  1048.8 50.7 %all-to-all-start.14 = ((f32[4,2,128,256]{3,1,2,0:T(2,128)}), f32[4,2,128,256]{3,1,2,0:T(2,128)S(1)}, u32[]{:S(2)}, u32[]{:S(2)}) async-start(f32[4,2,128,256]{3,1,2,0:T(2,128)} %broadcast_in_dim.23), calls=%async_computation.14 | async-start | bytes 2097152 | tf_op jit(solution)/shard_map/all_to_all | solution.py:42
  1052.5 116.5 %all-reduce.21.cloned.1.call-start = ((), (), s32[]{:S(2)}) async-start(), calls=%async_computation.20 | async-start | bytes 4194304 | tf_op jit(solution)/shard_map/psum | solution.py:110
  1100.6 68.4 %copy-start.3 = (f32[128,2048]{1,0:T(8,128)S(1)}, f32[128,2048]{1,0:T(8,128)}, u32[]{:S(2)}) copy-start(f32[128,2048]{1,0:T(8,128)} %copy-done.2) | copy-start | bytes 3145732
  1100.6 68.4 %copy-start.8 = (f32[128,2048]{1,0:T(8,128)S(1)}, f32[128,2048]{1,0:T(8,128)}, u32[]{:S(2)}) copy-start(f32[128,2048]{1,0:T(8,128)} %copy-done.7) | copy-start | bytes 3145732
  1100.6 33.0 %all-to-all-start.15 = ((f32[1,8,128,256]{3,2,0,1:T(8,128)}), f32[1,8,128,256]{3,2,0,1:T(8,128)S(1)}, u32[]{:S(2)}, u32[]{:S(2)}) async-start(f32[1,8,128,256]{3,2,0,1:T(8,128)} %bitcast.103), calls=%async_computation.15 | async-start | bytes 2097152 | tf_op jit(solution)/shard_map/all_to_all | solution.py:41
Sparse Core Ops, SparseCore 0:
  110.4 64.4 all-reduce.12
  402.6 64.4 all-reduce.14
  692.3 64.4 all-reduce.16
  982.1 64.4 all-reduce.18
Sparse Core Ops, SparseCore 1:
  228.5 69.2 all-reduce.26
  521.0 69.2 all-reduce.24
  810.5 69.2 all-reduce.22
  1099.6 69.3 all-reduce.20
where the time goes:
time: 1190 us; the launch traced here: 1180 us
  waiting for transfers between devices  392 us (33%)
  blocking collectives  333 us (28%)
  matrix products  330 us (28%)
  starting transfers between devices  51 us (4%)
  local copies, waits for them, and re-layouts  43.7 us (4%)
  between operations  16.1 us (1%)
  other arithmetic  14.3 us (1%)
    psum x4, waiting for transfers between devices, body(): cross_total = lax.psum(part_cross, 'col')  258 us
    all_to_all x4, blocking collectives, turn_rows(): lax.all_to_all(spread, 'col', split_axis=0, concat_axis=1, tiled=True)  216 us
    dot_general x4, matrix products, body(): lax.dot_general(slope_contribution, hist_resp, (((1,), (1,)), ((), ())),...  151 us
    psum x4, waiting for transfers between devices, body(): memory_corr, memory_resp = lax.psum((part_corr, part_resp), 'row')  133 us
    psum x4, blocking collectives, body(): enforcing_scalar_sum = lax.psum(multiplier_terms, 'col')  117 us
    dot_general x4, matrix products, body(): jnp.dot(energy_rows, hist_resp, precision=highest, preferred_element_type...  89.7 us
    dot_general x4, matrix products, body(): jnp.dot(energy_rows, hist_corr, precision=highest, preferred_element_type...  89.7 us
  transfers between devices with their start and end apart: 20, of which 8 were waited for; matrix products, arithmetic and copies ran while one was open for 31% of the time, Pallas kernels for 0%

commit v1 on v0

--- a/solution.py
+++ b/solution.py
@@ -1,3 +1,4 @@
+import functools
 import math
 import jax
 import jax.numpy as jnp
@@ -10,6 +11,38 @@
 heat_reservoir_warmth = 0.6
 
 
+def apply_the_islands(point, d0, base_x):
+    prior, a_next = (point.shape[:d0], point.shape[d0 + 1 :])
+    arr_now = jnp.moveaxis(point.reshape(*prior, base_x, -1, *a_next), d0, 0)
+    return arr_now
+
+
+def _balance_edge(local_block, where_dim):
+    local_block = jnp.moveaxis(local_block, 0, where_dim)
+    x_next = local_block.shape
+    oldest = local_block.reshape(
+        *x_next[:where_dim], x_next[where_dim] * x_next[where_dim + 1], *x_next[where_dim + 2 :]
+    )
+    return oldest
+
+
+def plan_series_all(page, ax_name, field, payload):
+    ready, then = (lax.axis_size(ax_name), lax.axis_index(ax_name))
+    val2 = apply_the_islands(page, field, ready)
+    arrivals = [val2[then]]
+    for at in range(1, ready):
+        current_value = val2[(then + at) % ready]
+        arrivals.append(
+            lax.ppermute(current_value, ax_name, [(pp, (pp + at) % ready) for pp in range(ready)])
+        )
+    val2 = jnp.stack(arrivals)[(then - jnp.arange(ready)) % ready]
+    item_now = _balance_edge(val2, payload)
+    return item_now
+
+
+_report_tracks = functools.partial(plan_series_all, ax_name="row", field=1, payload=0)
+
+
 def turn_rows(values):
     row_count = lax.axis_size("row")
     col_count = lax.axis_size("col")
@@ -17,13 +50,7 @@
     piece_span = values.shape[1] // row_count
     piece = lax.dynamic_slice_in_dim(values, my_row * piece_span, piece_span, 1)
     spread = jnp.broadcast_to(piece[None, None], (col_count, 1) + piece.shape)
-    moved = lax.all_to_all(
-        lax.all_to_all(spread, "col", split_axis=0, concat_axis=1, tiled=True),
-        "row",
-        split_axis=1,
-        concat_axis=0,
-        tiled=True,
-    )
+    moved = _report_tracks(lax.all_to_all(spread, "col", split_axis=0, concat_axis=1, tiled=True))
     return jnp.transpose(moved, (2, 1, 0, 3)).reshape(piece.shape[0], -1)
 
 

time: 1190 us -> 1000 us (0.84)
  blocking collectives: 333 us -> 117 us
  local copies, waits for them, and re-layouts: 43.7 us -> 71.2 us
  waiting for transfers between devices: 392 us -> 374 us
  starting transfers between devices: 51 us -> 66.5 us
    all_to_all x4 -> x0, blocking collectives: 216 us -> none  [turn_rows(): lax.all_to_all(spread, 'col', split_axis=0, concat_axis=1, tiled=True)]
    psum x4, waiting for transfers between devices: 258 us -> 207 us  [body(): cross_total = lax.psum(part_cross, 'col')]
    all_to_all x4, waiting for transfers between devices: 0.01 us -> 32.5 us  [turn_rows(): lax.all_to_all(spread, 'col', split_axis=0, concat_axis=1, tiled=True)]
    ppermute x0 -> x12, starting transfers between devices: none -> 13.7 us  [plan_series_all(): lax.ppermute(current_value, ax_name, [(pp, (pp + at) % ready) for pp in r...]
  transfers between devices with their start and end apart: 20 -> 32, of which waited for: 8 -> 12; matrix products, arithmetic and copies ran while one was open for 31% -> 40% of each run, Pallas kernels for 0% -> 0%
where the time goes in v1:
time: 1000 us; the launch traced here: 997 us
  waiting for transfers between devices  374 us (37%)
  matrix products  330 us (33%)
  blocking collectives  117 us (12%)
  local copies, waits for them, and re-layouts  71.2 us (7%)
  starting transfers between devices  66.5 us (7%)
  other arithmetic  21.5 us (2%)
  between operations  16.2 us (2%)
    psum x4, waiting for transfers between devices, body(): cross_total = lax.psum(part_cross, 'col')  207 us
    dot_general x4, matrix products, body(): lax.dot_general(slope_contribution, hist_resp, (((1,), (1,)), ((), ())),...  151 us
    psum x4, waiting for transfers between devices, body(): memory_corr, memory_resp = lax.psum((part_corr, part_resp), 'row')  134 us
    psum x4, blocking collectives, body(): enforcing_scalar_sum = lax.psum(multiplier_terms, 'col')  117 us
    dot_general x4, matrix products, body(): jnp.dot(energy_rows, hist_resp, precision=highest, preferred_element_type...  89.8 us
    dot_general x4, matrix products, body(): jnp.dot(energy_rows, hist_corr, precision=highest, preferred_element_type...  89.7 us
    all_to_all x4, waiting for transfers between devices, turn_rows(): lax.all_to_all(spread, 'col', split_axis=0, concat_axis=1, tiled=True)  32.5 us
    all_to_all x4, starting transfers between devices, turn_rows(): lax.all_to_all(spread, 'col', split_axis=0, concat_axis=1, tiled=True)  20.3 us
  transfers between devices with their start and end apart: 32, of which 12 were waited for; matrix products, arithmetic and copies ran while one was open for 40% of the time, Pallas kernels for 0%

profile of v1, /device:TPU:0, one launch (start us, length us, event | category | flops | bytes accessed | tf_op | source)
XLA Modules:
  0.0 996.8 jit_solution(3795585401593358550)
XLA Ops:
  11.6 6.5 all-to-all-start
  18.1 37.3 %fusion = f32[128,4096]{1,0:T(8,128)S(1)} fusion(f32[4096,2048]{1,0:T(8,128)} %param.5, f32[128,2048]{1,0:T(8,128)S(1)} %copy-done.4), kind=kOutput, calls=%fused_computation.28 | convolution fusion | flops 12885426176 | bytes 36700160 | tf_op jit(solution)/shard_map/dot_general | solution.py:117
  58.3 9.0 all-to-all-done
  73.5 51.4 %all-reduce.13.cloned.1.call-done = f32[128,2,2048]{2,1,0:T(2,128)} async-done(((f32[128,2,2048]{2,1,0:T(2,128)}), f32[128,2,2048]{2,1,0:T(2,128)}) %all-reduce.13.cloned.1.call-update) | async-done | bytes 2097168 | tf_op jit(solution)/shard_map/psum | solution.py:126
  138.4 22.4 %fusion.15 = f32[128,2048]{1,0:T(8,128)} fusion(f32[128,4096]{0,1:T(8,128)S(1)} %bitcast.118, f32[4096,2048]{1,0:T(8,128)} %param.5), kind=kOutput, calls=%fused_computation.76 | convolution fusion | flops 12884901888 | bytes 36700160 | tf_op jit(solution)/shard_map/dot_general | solution.py:134
  160.8 22.4 %fusion.14 = f32[128,2048]{1,0:T(8,128)} fusion(f32[128,4096]{0,1:T(8,128)S(1)} %bitcast.119, f32[4096,2048]{1,0:T(8,128)} %param.4), kind=kOutput, calls=%fused_computation.75 | convolution fusion | flops 12884901888 | bytes 36700160 | tf_op jit(solution)/shard_map/dot_general | solution.py:131
  189.3 29.3 %psum.114 = f32[128]{0:T(128)S(1)} all-reduce(f32[128]{0:T(128)S(1)} %get-tuple-element.36), channel_id=1, replica_groups=mesh['row'=4,'col'=8] {'col'}, use_global_device_ids=true, to_apply=%region_3.4 | all-reduce | flops 128 | bytes 1024 | tf_op jit(solution)/shard_map/psum | solution.py:124
  219.8 32.9 %all-reduce.27.cloned.1.call-done = (f32[128,2048]{1,0:T(8,128)}, f32[128,2048]{1,0:T(8,128)}) async-done(((f32[128,2048]{1,0:T(8,128)}, f32[128,2048]{1,0:T(8,128)}), (f32[128,2048]{1,0:T(8,128)}, f32[128,2048]{1,0:T(8,128)})) %all-reduce.27.cloned.1.call-update) | async-done | bytes 2097168 | tf_op jit(solution)/shard_map/psum | solution.py:137
  258.1 4.6 all-to-all-start.3
  263.0 39.0 %fusion.1 = f32[128,4096]{1,0:T(8,128)} fusion(f32[4096,2048]{1,0:T(8,128)} %param.5, f32[128,2048]{1,0:T(8,128)S(1)} %get-tuple-element.18), kind=kOutput, calls=%fused_computation.29 | convolution fusion | flops 12885426176 | bytes 36700160 | tf_op jit(solution)/shard_map/dot_general | solution.py:117
  306.0 5.9 all-to-all-done.3
  318.0 53.6 %all-reduce.15.cloned.1.call-done = f32[128,2,2048]{2,1,0:T(2,128)} async-done(((f32[128,2,2048]{2,1,0:T(2,128)}), f32[128,2,2048]{2,1,0:T(2,128)}) %all-reduce.15.cloned.1.call-update) | async-done | bytes 2097168 | tf_op jit(solution)/shard_map/psum | solution.py:126
  384.6 22.4 %fusion.17 = f32[128,2048]{1,0:T(8,128)} fusion(f32[128,4096]{0,1:T(8,128)S(1)} %bitcast.120, f32[4096,2048]{1,0:T(8,128)} %param.5), kind=kOutput, calls=%fused_computation.78 | convolution fusion | flops 12884901888 | bytes 36700160 | tf_op jit(solution)/shard_map/dot_general | solution.py:134
  407.1 22.4 %fusion.16 = f32[128,2048]{1,0:T(8,128)} fusion(f32[128,4096]{0,1:T(8,128)S(1)} %bitcast.121, f32[4096,2048]{1,0:T(8,128)} %param.4), kind=kOutput, calls=%fused_computation.77 | convolution fusion | flops 12884901888 | bytes 36700160 | tf_op jit(solution)/shard_map/dot_general | solution.py:131
  434.3 29.3 %psum.118 = f32[128]{0:T(128)S(1)} all-reduce(f32[128]{0:T(128)S(1)} %get-tuple-element.16), channel_id=1, replica_groups=mesh['row'=4,'col'=8] {'col'}, use_global_device_ids=true, to_apply=%region_8.9 | all-reduce | flops 128 | bytes 1024 | tf_op jit(solution)/shard_map/psum | solution.py:124
  464.7 34.2 %all-reduce.25.cloned.1.call-done = (f32[128,2048]{1,0:T(8,128)}, f32[128,2048]{1,0:T(8,128)}) async-done(((f32[128,2048]{1,0:T(8,128)}, f32[128,2048]{1,0:T(8,128)}), (f32[128,2048]{1,0:T(8,128)}, f32[128,2048]{1,0:T(8,128)})) %all-reduce.25.cloned.1.call-update) | async-done | bytes 2097168 | tf_op jit(solution)/shard_map/psum | solution.py:137
  503.8 4.6 all-to-all-start.6
  508.6 37.2 %fusion.2 = f32[128,4096]{1,0:T(8,128)S(1)} fusion(f32[4096,2048]{1,0:T(8,128)} %param.5, f32[128,2048]{1,0:T(8,128)S(1)} %get-tuple-element.15), kind=kOutput, calls=%fused_computation.30 | convolution fusion | flops 12885426176 | bytes 36700160 | tf_op jit(solution)/shard_map/dot_general | solution.py:117
  548.7 8.9 all-to-all-done.6
  563.7 50.8 %all-reduce.17.cloned.1.call-done = f32[128,2,2048]{2,1,0:T(2,128)} async-done(((f32[128,2,2048]{2,1,0:T(2,128)}), f32[128,2,2048]{2,1,0:T(2,128)}) %all-reduce.17.cloned.1.call-update) | async-done | bytes 2097168 | tf_op jit(solution)/shard_map/psum | solution.py:126
  628.0 22.5 %fusion.19 = f32[128,2048]{1,0:T(8,128)} fusion(f32[128,4096]{0,1:T(8,128)S(1)} %bitcast.122, f32[4096,2048]{1,0:T(8,128)} %param.5), kind=kOutput, calls=%fused_computation.80 | convolution fusion | flops 12884901888 | bytes 36700160 | tf_op jit(solution)/shard_map/dot_general | solution.py:134
  650.4 22.4 %fusion.18 = f32[128,2048]{1,0:T(8,128)} fusion(f32[128,4096]{0,1:T(8,128)S(1)} %bitcast.123, f32[4096,2048]{1,0:T(8,128)} %param.4), kind=kOutput, calls=%fused_computation.79 | convolution fusion | flops 12884901888 | bytes 36700160 | tf_op jit(solution)/shard_map/dot_general | solution.py:131
  678.9 29.3 %psum.122 = f32[128]{0:T(128)S(1)} all-reduce(f32[128]{0:T(128)S(1)} %get-tuple-element.13), channel_id=1, replica_groups=mesh['row'=4,'col'=8] {'col'}, use_global_device_ids=true, to_apply=%region_13.14 | all-reduce | flops 128 | bytes 1024 | tf_op jit(solution)/shard_map/psum | solution.py:124
  709.3 32.9 %all-reduce.23.cloned.1.call-done = (f32[128,2048]{1,0:T(8,128)}, f32[128,2048]{1,0:T(8,128)}) async-done(((f32[128,2048]{1,0:T(8,128)}, f32[128,2048]{1,0:T(8,128)}), (f32[128,2048]{1,0:T(8,128)}, f32[128,2048]{1,0:T(8,128)})) %all-reduce.23.cloned.1.call-update) | async-done | bytes 2097168 | tf_op jit(solution)/shard_map/psum | solution.py:137
  747.7 4.6 all-to-all-start.9
  752.8 37.2 %fusion.3 = f32[128,4096]{1,0:T(8,128)S(1)} fusion(f32[4096,2048]{1,0:T(8,128)} %param.5, f32[128,2048]{1,0:T(8,128)S(1)} %get-tuple-element.12), kind=kOutput, calls=%fused_computation.31 | convolution fusion | flops 12885426176 | bytes 36700160 | tf_op jit(solution)/shard_map/dot_general | solution.py:117
  792.8 8.7 all-to-all-done.9
  807.4 51.2 %all-reduce.19.cloned.1.call-done = f32[128,2,2048]{2,1,0:T(2,128)} async-done(((f32[128,2,2048]{2,1,0:T(2,128)}), f32[128,2,2048]{2,1,0:T(2,128)}) %all-reduce.19.cloned.1.call-update) | async-done | bytes 2097168 | tf_op jit(solution)/shard_map/psum | solution.py:126
  871.2 22.4 %fusion.21 = f32[128,2048]{1,0:T(8,128)} fusion(f32[128,4096]{0,1:T(8,128)S(1)} %bitcast.124, f32[4096,2048]{1,0:T(8,128)} %param.5), kind=kOutput, calls=%fused_computation.82 | convolution fusion | flops 12884901888 | bytes 36700160 | tf_op jit(solution)/shard_map/dot_general | solution.py:134
  893.6 22.4 %fusion.20 = f32[128,2048]{1,0:T(8,128)} fusion(f32[128,4096]{0,1:T(8,128)S(1)} %bitcast.125, f32[4096,2048]{1,0:T(8,128)} %param.4), kind=kOutput, calls=%fused_computation.81 | convolution fusion | flops 12884901888 | bytes 36700160 | tf_op jit(solution)/shard_map/dot_general | solution.py:131
  920.8 29.3 %psum.126 = f32[128]{0:T(128)S(1)} all-reduce(f32[128]{0:T(128)S(1)} %get-tuple-element.10), channel_id=1, replica_groups=mesh['row'=4,'col'=8] {'col'}, use_global_device_ids=true, to_apply=%region_18.19 | all-reduce | flops 128 | bytes 1024 | tf_op jit(solution)/shard_map/psum | solution.py:124
  951.3 34.3 %all-reduce.21.cloned.1.call-done = (f32[128,2048]{1,0:T(8,128)}, f32[128,2048]{1,0:T(8,128)}) async-done(((f32[128,2048]{1,0:T(8,128)}, f32[128,2048]{1,0:T(8,128)}), (f32[128,2048]{1,0:T(8,128)}, f32[128,2048]{1,0:T(8,128)})) %all-reduce.21.cloned.1.call-update) | async-done | bytes 2097168 | tf_op jit(solution)/shard_map/psum | solution.py:137
  (150 shorter events, 139.1 us)
Async XLA Ops:
  11.6 55.6 %all-to-all-start = ((f32[8,1,128,512]{3,2,1,0:T(8,128)}), f32[8,1,128,512]{3,2,1,0:T(8,128)}, u32[]{:S(2)}, u32[]{:S(2)}) async-start(f32[8,1,128,512]{3,2,1,0:T(8,128)} %broadcast_in_dim.16), calls=%async_computation | async-start | bytes 4194304 | tf_op jit(solution)/shard_map/all_to_all | solution.py:53
  18.1 106.9 %all-reduce.13.cloned.1.call-start = ((), (), s32[]{:S(2)}) async-start(), calls=%async_computation.12 | async-start | bytes 4194304 | tf_op jit(solution)/shard_map/psum | solution.py:126
  70.0 61.7 %collective-permute-start.2 = (f32[1,2,128,512]{3,2,1,0:T(8,128)}, f32[1,2,128,512]{3,2,1,0:T(8,128)S(1)}, u32[]{:S(2)}, u32[]{:S(2)}) collective-permute-start(f32[1,2,128,512]{3,2,1,0:T(8,128)} %get-tuple-element.32), channel_id=1, source_target_pairs={{0,24},{8,0},{16,8},{24,16},{1,25},{9,1},{17,9},{25,17},{2,26},{10... | collective-permute-start | bytes 1572872 | tf_op jit(solution)/shard_map/ppermute | solution.py:36
  72.4 59.3 %collective-permute-start.1 = (f32[1,2,128,512]{3,2,1,0:T(8,128)S(1)}, f32[1,2,128,512]{3,2,1,0:T(8,128)S(1)}, u32[]{:S(2)}, u32[]{:S(2)}) collective-permute-start(f32[1,2,128,512]{3,2,1,0:T(8,128)S(1)} %get-tuple-element.33), channel_id=1, source_target_pairs={{0,16},{8,24},{16,0},{24,8},{1,17},{9,25},{17,1},{25,9},{2,18},{10... | collective-permute-start | bytes 1572872 | tf_op jit(solution)/shard_map/ppermute | solution.py:36
  72.9 58.8 %collective-permute-start = (f32[1,2,128,512]{3,2,1,0:T(8,128)S(1)}, f32[1,2,128,512]{3,2,1,0:T(8,128)}, u32[]{:S(2)}, u32[]{:S(2)}) collective-permute-start(f32[1,2,128,512]{3,2,1,0:T(8,128)S(1)} %get-tuple-element.34), channel_id=1, source_target_pairs={{0,8},{8,16},{16,24},{24,0},{1,9},{9,17},{17,25},{25,1},{2,10},{10... | collective-permute-start | bytes 1572872 | tf_op jit(solution)/shard_map/ppermute | solution.py:36
  127.2 56.1 %all-to-all-start.1 = ((f32[4,2,128,256]{3,1,2,0:T(2,128)}), f32[4,2,128,256]{3,1,2,0:T(2,128)}, u32[]{:S(2)}, u32[]{:S(2)}) async-start(f32[4,2,128,256]{3,1,2,0:T(2,128)} %broadcast_in_dim.17), calls=%async_computation.1 | async-start | bytes 2097152 | tf_op jit(solution)/shard_map/all_to_all | solution.py:69
  131.5 121.2 %all-reduce.27.cloned.1.call-start = ((), (), s32[]{:S(2)}) async-start(), calls=%async_computation.19 | async-start | bytes 4194304 | tf_op jit(solution)/shard_map/psum | solution.py:137
  185.6 33.0 %all-to-all-start.2 = ((f32[1,8,128,256]{3,2,0,1:T(8,128)}), f32[1,8,128,256]{3,2,0,1:T(8,128)S(1)}, u32[]{:S(2)}, u32[]{:S(2)}) async-start(f32[1,8,128,256]{3,2,0,1:T(8,128)} %bitcast.13), calls=%async_computation.2 | async-start | bytes 2097152 | tf_op jit(solution)/shard_map/all_to_all | solution.py:68
  258.1 53.7 %all-to-all-start.3 = ((f32[8,1,128,512]{3,2,1,0:T(8,128)}), f32[8,1,128,512]{3,2,1,0:T(8,128)}, u32[]{:S(2)}, u32[]{:S(2)}) async-start(f32[8,1,128,512]{3,2,1,0:T(8,128)} %broadcast_in_dim.18), calls=%async_computation.3 | async-start | bytes 4194304 | tf_op jit(solution)/shard_map/all_to_all | solution.py:53
  262.7 108.9 %all-reduce.15.cloned.1.call-start = ((), (), s32[]{:S(2)}) async-start(), calls=%async_computation.13 | async-start | bytes 4194304 | tf_op jit(solution)/shard_map/psum | solution.py:126
  314.6 63.3 %collective-permute-start.5 = (f32[1,2,128,512]{3,2,1,0:T(8,128)}, f32[1,2,128,512]{3,2,1,0:T(8,128)S(1)}, u32[]{:S(2)}, u32[]{:S(2)}) collective-permute-start(f32[1,2,128,512]{3,2,1,0:T(8,128)} %get-tuple-element.28), channel_id=1, source_target_pairs={{0,24},{8,0},{16,8},{24,16},{1,25},{9,1},{17,9},{25,17},{2,26},{10... | collective-permute-start | bytes 1572872 | tf_op jit(solution)/shard_map/ppermute | solution.py:36
  316.2 61.7 %collective-permute-start.4 = (f32[1,2,128,512]{3,2,1,0:T(8,128)S(1)}, f32[1,2,128,512]{3,2,1,0:T(8,128)S(1)}, u32[]{:S(2)}, u32[]{:S(2)}) collective-permute-start(f32[1,2,128,512]{3,2,1,0:T(8,128)S(1)} %get-tuple-element.29), channel_id=1, source_target_pairs={{0,16},{8,24},{16,0},{24,8},{1,17},{9,25},{17,1},{25,9},{2,18},{10... | collective-permute-start | bytes 1572872 | tf_op jit(solution)/shard_map/ppermute | solution.py:36
  317.6 60.3 %collective-permute-start.3 = (f32[1,2,128,512]{3,2,1,0:T(8,128)S(1)}, f32[1,2,128,512]{3,2,1,0:T(8,128)}, u32[]{:S(2)}, u32[]{:S(2)}) collective-permute-start(f32[1,2,128,512]{3,2,1,0:T(8,128)S(1)} %get-tuple-element.30), channel_id=1, source_target_pairs={{0,8},{8,16},{16,24},{24,0},{1,9},{9,17},{17,25},{25,1},{2,10},{10... | collective-permute-start | bytes 1572872 | tf_op jit(solution)/shard_map/ppermute | solution.py:36
  373.8 55.7 %all-to-all-start.4 = ((f32[4,2,128,256]{3,1,2,0:T(2,128)}), f32[4,2,128,256]{3,1,2,0:T(2,128)S(1)}, u32[]{:S(2)}, u32[]{:S(2)}) async-start(f32[4,2,128,256]{3,1,2,0:T(2,128)} %broadcast_in_dim.19), calls=%async_computation.4 | async-start | bytes 2097152 | tf_op jit(solution)/shard_map/all_to_all | solution.py:69
  377.5 121.5 %all-reduce.25.cloned.1.call-start = ((), (), s32[]{:S(2)}) async-start(), calls=%async_computation.18 | async-start | bytes 4194304 | tf_op jit(solution)/shard_map/psum | solution.py:137
  430.6 33.0 %all-to-all-start.5 = ((f32[1,8,128,256]{3,2,0,1:T(8,128)}), f32[1,8,128,256]{3,2,0,1:T(8,128)S(1)}, u32[]{:S(2)}, u32[]{:S(2)}) async-start(f32[1,8,128,256]{3,2,0,1:T(8,128)} %bitcast.134), calls=%async_computation.5 | async-start | bytes 2097152 | tf_op jit(solution)/shard_map/all_to_all | solution.py:68
  503.8 53.8 %all-to-all-start.6 = ((f32[8,1,128,512]{3,2,1,0:T(8,128)}), f32[8,1,128,512]{3,2,1,0:T(8,128)}, u32[]{:S(2)}, u32[]{:S(2)}) async-start(f32[8,1,128,512]{3,2,1,0:T(8,128)} %broadcast_in_dim.20), calls=%async_computation.6 | async-start | bytes 4194304 | tf_op jit(solution)/shard_map/all_to_all | solution.py:53
  508.4 106.1 %all-reduce.17.cloned.1.call-start = ((), (), s32[]{:S(2)}) async-start(), calls=%async_computation.14 | async-start | bytes 4194304 | tf_op jit(solution)/shard_map/psum | solution.py:126
  560.3 60.9 %collective-permute-start.8 = (f32[1,2,128,512]{3,2,1,0:T(8,128)}, f32[1,2,128,512]{3,2,1,0:T(8,128)S(1)}, u32[]{:S(2)}, u32[]{:S(2)}) collective-permute-start(f32[1,2,128,512]{3,2,1,0:T(8,128)} %get-tuple-element.24), channel_id=1, source_target_pairs={{0,24},{8,0},{16,8},{24,16},{1,25},{9,1},{17,9},{25,17},{2,26},{10... | collective-permute-start | bytes 1572872 | tf_op jit(solution)/shard_map/ppermute | solution.py:36
  561.7 59.5 %collective-permute-start.7 = (f32[1,2,128,512]{3,2,1,0:T(8,128)S(1)}, f32[1,2,128,512]{3,2,1,0:T(8,128)S(1)}, u32[]{:S(2)}, u32[]{:S(2)}) collective-permute-start(f32[1,2,128,512]{3,2,1,0:T(8,128)S(1)} %get-tuple-element.25), channel_id=1, source_target_pairs={{0,16},{8,24},{16,0},{24,8},{1,17},{9,25},{17,1},{25,9},{2,18},{10... | collective-permute-start | bytes 1572872 | tf_op jit(solution)/shard_map/ppermute | solution.py:36
  563.3 58.0 %collective-permute-start.6 = (f32[1,2,128,512]{3,2,1,0:T(8,128)S(1)}, f32[1,2,128,512]{3,2,1,0:T(8,128)}, u32[]{:S(2)}, u32[]{:S(2)}) collective-permute-start(f32[1,2,128,512]{3,2,1,0:T(8,128)S(1)} %get-tuple-element.26), channel_id=1, source_target_pairs={{0,8},{8,16},{16,24},{24,0},{1,9},{9,17},{17,25},{25,1},{2,10},{10... | collective-permute-start | bytes 1572872 | tf_op jit(solution)/shard_map/ppermute | solution.py:36
  616.7 56.2 %all-to-all-start.7 = ((f32[4,2,128,256]{3,1,2,0:T(2,128)}), f32[4,2,128,256]{3,1,2,0:T(2,128)}, u32[]{:S(2)}, u32[]{:S(2)}) async-start(f32[4,2,128,256]{3,1,2,0:T(2,128)} %broadcast_in_dim.21), calls=%async_computation.7 | async-start | bytes 2097152 | tf_op jit(solution)/shard_map/all_to_all | solution.py:69
  620.9 121.3 %all-reduce.23.cloned.1.call-start = ((), (), s32[]{:S(2)}) async-start(), calls=%async_computation.17 | async-start | bytes 4194304 | tf_op jit(solution)/shard_map/psum | solution.py:137
  675.2 33.0 %all-to-all-start.8 = ((f32[1,8,128,256]{3,2,0,1:T(8,128)}), f32[1,8,128,256]{3,2,0,1:T(8,128)S(1)}, u32[]{:S(2)}, u32[]{:S(2)}) async-start(f32[1,8,128,256]{3,2,0,1:T(8,128)} %bitcast.135), calls=%async_computation.8 | async-start | bytes 2097152 | tf_op jit(solution)/shard_map/all_to_all | solution.py:68
  747.7 53.8 %all-to-all-start.9 = ((f32[8,1,128,512]{3,2,1,0:T(8,128)}), f32[8,1,128,512]{3,2,1,0:T(8,128)}, u32[]{:S(2)}, u32[]{:S(2)}) async-start(f32[8,1,128,512]{3,2,1,0:T(8,128)} %broadcast_in_dim.22), calls=%async_computation.9 | async-start | bytes 4194304 | tf_op jit(solution)/shard_map/all_to_all | solution.py:53
  752.3 106.3 %all-reduce.19.cloned.1.call-start = ((), (), s32[]{:S(2)}) async-start(), calls=%async_computation.15 | async-start | bytes 4194304 | tf_op jit(solution)/shard_map/psum | solution.py:126
  804.1 60.6 %collective-permute-start.11 = (f32[1,2,128,512]{3,2,1,0:T(8,128)S(1)}, f32[1,2,128,512]{3,2,1,0:T(8,128)S(1)}, u32[]{:S(2)}, u32[]{:S(2)}) collective-permute-start(f32[1,2,128,512]{3,2,1,0:T(8,128)S(1)} %get-tuple-element.20), channel_id=1, source_target_pairs={{0,24},{8,0},{16,8},{24,16},{1,25},{9,1},{17,9},{25,17},{2,26},{10... | collective-permute-start | bytes 1572872 | tf_op jit(solution)/shard_map/ppermute | solution.py:36
  805.5 59.2 %collective-permute-start.10 = (f32[1,2,128,512]{3,2,1,0:T(8,128)S(1)}, f32[1,2,128,512]{3,2,1,0:T(8,128)}, u32[]{:S(2)}, u32[]{:S(2)}) collective-permute-start(f32[1,2,128,512]{3,2,1,0:T(8,128)S(1)} %get-tuple-element.21), channel_id=1, source_target_pairs={{0,16},{8,24},{16,0},{24,8},{1,17},{9,25},{17,1},{25,9},{2,18},{10... | collective-permute-start | bytes 1572872 | tf_op jit(solution)/shard_map/ppermute | solution.py:36
  807.0 57.7 %collective-permute-start.9 = (f32[1,2,128,512]{3,2,1,0:T(8,128)S(1)}, f32[1,2,128,512]{3,2,1,0:T(8,128)}, u32[]{:S(2)}, u32[]{:S(2)}) collective-permute-start(f32[1,2,128,512]{3,2,1,0:T(8,128)S(1)} %get-tuple-element.22), channel_id=1, source_target_pairs={{0,8},{8,16},{16,24},{24,0},{1,9},{9,17},{17,25},{25,1},{2,10},{10... | collective-permute-start | bytes 1572872 | tf_op jit(solution)/shard_map/ppermute | solution.py:36
  860.8 55.3 %all-to-all-start.10 = ((f32[4,2,128,256]{3,1,2,0:T(2,128)}), f32[4,2,128,256]{3,1,2,0:T(2,128)S(1)}, u32[]{:S(2)}, u32[]{:S(2)}) async-start(f32[4,2,128,256]{3,1,2,0:T(2,128)} %broadcast_in_dim.23), calls=%async_computation.10 | async-start | bytes 2097152 | tf_op jit(solution)/shard_map/all_to_all | solution.py:69
  864.4 121.1 %all-reduce.21.cloned.1.call-start = ((), (), s32[]{:S(2)}) async-start(), calls=%async_computation.16 | async-start | bytes 4194304 | tf_op jit(solution)/shard_map/psum | solution.py:137
  917.1 33.0 %all-to-all-start.11 = ((f32[1,8,128,256]{3,2,0,1:T(8,128)}), f32[1,8,128,256]{3,2,0,1:T(8,128)S(1)}, u32[]{:S(2)}, u32[]{:S(2)}) async-start(f32[1,8,128,256]{3,2,0,1:T(8,128)} %bitcast.136), calls=%async_computation.11 | async-start | bytes 2097152 | tf_op jit(solution)/shard_map/all_to_all | solution.py:68
  (18 other events, 371.3 us)
Sparse Core Ops, SparseCore 0:
  58.3 66.5 all-reduce.12
  306.1 65.4 all-reduce.14
  548.8 65.6 all-reduce.16
  793.0 65.5 all-reduce.18
Sparse Core Ops, SparseCore 1:
  183.4 69.2 all-reduce.26
  429.6 69.3 all-reduce.24
  673.0 69.2 all-reduce.22
  916.1 69.3 all-reduce.20
